TPU v7x, 32 devices: a whole 2x2x4 slice. The times are simulated.
32 devices in a mesh: inst: 4 (over z), shard: 8 (over y, x, core).
Axes of the slice: x: 2, y: 2, z: 4, core: 2. Of those that a mesh axis runs over, the one named last changes fastest.
Arguments:
- master_old: float32 [4, 16, 65536], P('inst', 'shard'), may hold values from -3 to 3
- first_old: float32 [4, 16, 65536], P('inst', 'shard'), may hold values from -2 to 2
- second_old: float32 [4, 16, 65536], P('inst', 'shard'), may hold values from 0.01 to 1
- healthy: int32 [8], replicated, may hold values from 0 to 3
- slice_table: int32 [16], replicated, may hold values from 0 to 15, as said below
Outputs:
- master_new: float32 [4, 16, 65536], P('inst', 'shard')
- first_new: float32 [4, 16, 65536], P('inst', 'shard')
- second_new: float32 [4, 16, 65536], P('inst', 'shard')
- params_half: bfloat16 [4, 16, 65536], P('inst', 'shard')
- checksum: float32 [4, 2], P('inst')
Inputs may be any that keep to these rules, and one draw needn't show every extreme that they name: slice_table[k] = (k + slice_table[0]) mod 16 for every k, with slice_table[0] odd and at least 3.
All inputs are finite; a program needn't handle non-finite values.
Results may differ from a plain program's by a relative error of at most 0.001.
Values sent between devices are 32-bit elements; how exact they have to be, the bound alone decides.
No kernel may reach another device: no remote copies, remote signals or barrier semaphores. Data moves between devices by JAX's collectives and lax.ppermute only.
A program may use at most 64 MiB of HBM per device.

v0:
```python
import jax
import jax.numpy as jnp
from jax import lax
from jax.sharding import PartitionSpec as P


def passed_along(value, axis, steps):
    count = lax.axis_size(axis)
    pairs = [(source, (source + steps) % count) for source in range(count)]
    return lax.ppermute(value, axis, pairs)


def from_root(block, axis, owner):
    block = jnp.where(lax.axis_index(axis) == owner, block, jnp.zeros_like(block))
    return lax.psum(block, axis)


def position_keys(flat_rows, columns):
    residue = flat_rows * (columns % 101) % 101
    offsets = jnp.arange(columns, dtype=jnp.int32)
    cycled = (residue[:, None] + offsets[None, :]) % 101
    return (cycled * 37 % 101 + 1).astype(jnp.float32) / 101.0


def weighted(master, first_moment, second, flat_rows):
    weights = position_keys(flat_rows, master.shape[2])
    combined = master[0] + first_moment[0] + second[0]
    return jnp.stack([jnp.sum(combined * weights), jnp.sum(master[0] * weights)])


def grand_total(partial_value):
    return lax.psum(partial_value, "shard")


def join_parts(pieces):
    return (
        lax.all_gather(pieces[0], "inst", axis=2, tiled=True),
        lax.all_gather(pieces[1], "inst", axis=2, tiled=True),
        lax.all_gather(pieces[2], "inst", axis=2, tiled=True),
    )


def reorder(arrays, rotation, owners):
    for bit_level in range((owners - 1).bit_length()):
        shifted = passed_along((arrays[0], arrays[1], arrays[2]), "shard", 1 << bit_level)
        chosen = rotation >> bit_level & 1 == 1
        arrays = tuple(
            (
                jnp.where(chosen, shifted_one, current)
                for shifted_one, current in zip(shifted, arrays)
            )
        )
    carried = passed_along((arrays[0][:, 1:2], arrays[1][:, 1:2], arrays[2][:, 1:2]), "shard", 1)
    return tuple(
        (
            jnp.concatenate([carried_one, current[:, 0:1]], axis=1)
            for carried_one, current in zip(carried, arrays)
        )
    )


def on_device(master_old, first_old, second_old, healthy, slice_table):
    source_index = lax.dynamic_index_in_dim(healthy, lax.axis_index("shard"), 0, keepdims=False)
    owners = lax.axis_size("shard")
    instances = lax.axis_size("inst")
    columns = master_old.shape[2]
    part_len = columns // instances
    normalizer = 1.0 / (2.0 * columns)
    rotation = slice_table[0] // 2
    master, first_moment, second = (
        from_root(master_old, "inst", source_index),
        from_root(first_old, "inst", source_index),
        from_root(second_old, "inst", source_index),
    )
    offset_start = lax.axis_index("inst") * part_len
    pieces = tuple(
        (
            lax.dynamic_slice_in_dim(stacked, offset_start, part_len, 2)
            for stacked in (master, first_moment, second)
        )
    )
    pieces = reorder(pieces, rotation, owners)
    master, first_moment, second = join_parts(pieces)
    new_rows = 2 * lax.axis_index("shard") + jnp.arange(2, dtype=jnp.int32)
    checksum = grand_total(weighted(master, first_moment, second, new_rows))
    checksum = jnp.reshape(checksum * normalizer, (1, 2))
    return (master, first_moment, second, master.astype(jnp.bfloat16), checksum)


def solution(mesh):
    placed = (
        P("inst", "shard", None),
        P("inst", "shard", None),
        P("inst", "shard", None),
        P(),
        P(),
    )
    return jax.shard_map(
        on_device,
        mesh=mesh,
        in_specs=placed,
        out_specs=(
            P("inst", "shard", None),
            P("inst", "shard", None),
            P("inst", "shard", None),
            P("inst", "shard", None),
            P("inst", None),
        ),
        check_vma=False,
    )
```

profile of v0, /device:TPU:0, one launch (start us, length us, event | category | flops | bytes accessed | tf_op | source)
XLA Modules:
  0.0 187.4 jit_solution(15723886663687752897)
XLA Ops:
  9.1 2.1 %broadcast_select_fusion.2 = f32[1,2,65536]{2,1,0:T(2,128)} fusion(f32[1,2,65536]{2,1,0:T(2,128)} %param.5, pred[]{:T(512)S(6)} %eq.22), kind=kLoop, calls=%fused_computation.15 | loop fusion | flops 131072 | bytes 1048577 | tf_op jit(solution)/shard_map/jit(_where)/select_n | solution.py:14
  11.3 1.5 broadcast_select_fusion
  13.7 70.2 %all-reduce.3.cloned.1.call-done = (f32[1,2,65536]{2,1,0:T(2,128)}, f32[1,2,65536]{2,1,0:T(2,128)}, f32[1,2,65536]{2,1,0:T(2,128)}) async-done(((f32[1,2,65536]{2,1,0:T(2,128)}, f32[1,2,65536]{2,1,0:T(2,128)}, f32[1,2,65536]{2,1,0:T(2,128)}), (f32[1,2,65536]{2,1,0:T(2,128)}, f32[1,2,65536]{2,1,0:T(2,128)}, f32[1,2,65536]{2,1,0:T(2,128)})) %all-reduce.3.cloned.1.call-update) | async-done | bytes 1572880 | tf_op jit(solution)/shard_map/psum | solution.py:15
  83.9 1.0 constant_dynamic-slice_fusion
  84.9 0.9 constant_dynamic-slice_fusion.1
  85.8 1.6 collective-permute-start.4
  87.6 2.6 %collective-permute-done.8 = f32[1,2,16384]{2,1,0:T(2,128)S(1)} collective-permute-done((f32[1,2,16384]{2,1,0:T(2,128)S(1)}, f32[1,2,16384]{2,1,0:T(2,128)S(1)}, u32[]{:S(2)}, u32[]{:S(2)}) %collective-permute-start.8) | collective-permute-done | bytes 131104 | tf_op jit(solution)/shard_map/ppermute | solution.py:10
  90.2 1.0 broadcast_select_fusion.3
  91.8 1.0 broadcast_select_fusion.4
  92.8 2.4 %collective-permute-start.5 = (f32[1,2,16384]{2,1,0:T(2,128)S(1)}, f32[1,2,16384]{2,1,0:T(2,128)S(1)}, u32[]{:S(2)}, u32[]{:S(2)}) collective-permute-start(f32[1,2,16384]{2,1,0:T(2,128)S(1)} %broadcast_select_fusion.4), channel_id=1, source_target_pairs={{0,2},{1,3},{2,4},{3,5},{4,6},{5,7},{6,0},{7,1},{8,10},{9,11},{10,... | collective-permute-start | bytes 393224 | tf_op jit(solution)/shard_map/ppermute | solution.py:10
  95.9 2.5 %collective-permute-done.9 = f32[1,2,16384]{2,1,0:T(2,128)S(1)} collective-permute-done((f32[1,2,16384]{2,1,0:T(2,128)S(1)}, f32[1,2,16384]{2,1,0:T(2,128)S(1)}, u32[]{:S(2)}, u32[]{:S(2)}) %collective-permute-start.9) | collective-permute-done | bytes 131104 | tf_op jit(solution)/shard_map/ppermute | solution.py:10
  98.5 1.7 collective-permute-start.10
  100.2 1.0 collective-permute-done.5
  101.3 1.0 collective-permute-start.6
  103.7 1.9 %collective-permute-done.10 = f32[1,2,16384]{2,1,0:T(2,128)S(1)} collective-permute-done((f32[1,2,16384]{2,1,0:T(2,128)S(1)}, f32[1,2,16384]{2,1,0:T(2,128)S(1)}, u32[]{:S(2)}, u32[]{:S(2)}) %collective-permute-start.10) | collective-permute-done | bytes 131104 | tf_op jit(solution)/shard_map/ppermute | solution.py:10
  105.9 2.6 %collective-permute-done.6 = f32[1,2,16384]{2,1,0:T(2,128)S(1)} collective-permute-done((f32[1,2,16384]{2,1,0:T(2,128)S(1)}, f32[1,2,16384]{2,1,0:T(2,128)S(1)}, u32[]{:S(2)}, u32[]{:S(2)}) %collective-permute-start.6) | collective-permute-done | bytes 131104 | tf_op jit(solution)/shard_map/ppermute | solution.py:10
  108.7 3.2 %collective-permute-done.2 = f32[1,2,16384]{2,1,0:T(2,128)S(1)} collective-permute-done((f32[1,2,16384]{2,1,0:T(2,128)S(1)}, f32[1,2,16384]{2,1,0:T(2,128)S(1)}, u32[]{:S(2)}, u32[]{:S(2)}) %collective-permute-start.2) | collective-permute-done | bytes 131104 | tf_op jit(solution)/shard_map/ppermute | solution.py:10
  112.2 16.1 %all_gather.11 = f32[1,2,65536]{2,1,0:T(2,128)S(1)} all-gather(f32[1,2,16384]{2,1,0:T(2,128)S(1)} %pad_maximum_fusion.2), channel_id=1, replica_groups=mesh['inst'=4,'shard'=8] {'inst'}, dimensions={2}, use_global_device_ids=true | all-gather | bytes 655360 | tf_op jit(solution)/shard_map/all_gather | solution.py:39
  128.4 15.8 %all_gather.10 = f32[1,2,65536]{2,1,0:T(2,128)S(1)} all-gather(f32[1,2,16384]{2,1,0:T(2,128)S(1)} %pad_maximum_fusion.1), channel_id=1, replica_groups=mesh['inst'=4,'shard'=8] {'inst'}, dimensions={2}, use_global_device_ids=true | all-gather | bytes 655360 | tf_op jit(solution)/shard_map/all_gather | solution.py:38
  144.3 15.0 %all_gather.9 = f32[1,2,65536]{2,1,0:T(2,128)S(1)} all-gather(f32[1,2,16384]{2,1,0:T(2,128)S(1)} %pad_maximum_fusion), channel_id=1, replica_groups=mesh['inst'=4,'shard'=8] {'inst'}, dimensions={2}, use_global_device_ids=true | all-gather | bytes 655360 | tf_op jit(solution)/shard_map/all_gather | solution.py:37
  159.3 4.3 %fusion.6 = (f32[]{:T(128)}, f32[]{:T(128)}) fusion(f32[1,2,65536]{2,1,0:T(2,128)S(1)} %all_gather.11, f32[1,2,65536]{2,1,0:T(2,128)S(1)} %all_gather.10, f32[1,2,65536]{2,1,0:T(2,128)S(1)} %all_gather.9, s32[2]{0:T(128)S(1)} %and_select_fusion.2), kind=kLoop, calls=%fused_computation.9 | loop fusion | flops 3014654 | bytes 1572880 | tf_op jit(solution)/shard_map/reduce_sum | solution.py:28
  163.6 1.4 pad_maximum_fusion.3
  165.0 0.9 convert_element_type.6
  165.9 11.8 %psum.31 = f32[2]{0:T(128)S(1)} all-reduce(f32[2]{0:T(128)S(1)} %pad_maximum_fusion.3), channel_id=1, replica_groups=mesh['inst'=4,'shard'=8] {'shard'}, use_global_device_ids=true, to_apply=%region_5.6 | all-reduce | flops 2 | bytes 16 | tf_op jit(solution)/shard_map/psum | solution.py:32
  (46 shorter events, 8.9 us)
Async XLA Ops:
  7.2 76.7 %all-reduce.3.cloned.1.call-start = ((), (), s32[]{:S(2)}) async-start(), calls=%async_computation | async-start | bytes 3145728 | tf_op jit(solution)/shard_map/psum | solution.py:15
  7.2 0.7 copy-start.4
  9.1 2.2 %copy-start = (f32[1,2,65536]{2,1,0:T(2,128)S(1)}, f32[1,2,65536]{2,1,0:T(2,128)}, u32[]{:S(2)}) copy-start(f32[1,2,65536]{2,1,0:T(2,128)} %param.7) | copy-start | bytes 1572868
  9.1 2.2 %copy-start.1 = (f32[1,2,65536]{2,1,0:T(2,128)S(1)}, f32[1,2,65536]{2,1,0:T(2,128)}, u32[]{:S(2)}) copy-start(f32[1,2,65536]{2,1,0:T(2,128)} %param.6) | copy-start | bytes 1572868
  12.8 0.7 copy-start.3
  83.9 3.6 %copy-start.2 = (f32[1,2,65536]{2,1,0:T(2,128)S(1)}, f32[1,2,65536]{2,1,0:T(2,128)}, u32[]{:S(2)}) copy-start(f32[1,2,65536]{2,1,0:T(2,128)} %get-tuple-element.7) | copy-start | bytes 1572868
  84.9 5.3 %collective-permute-start.8 = (f32[1,2,16384]{2,1,0:T(2,128)S(1)}, f32[1,2,16384]{2,1,0:T(2,128)S(1)}, u32[]{:S(2)}, u32[]{:S(2)}) collective-permute-start(f32[1,2,16384]{2,1,0:T(2,128)S(1)} %constant_dynamic-slice_fusion), channel_id=1, source_target_pairs={{0,1},{1,2},{2,3},{3,4},{4,5},{5,6},{6,7},{7,0},{8,9},{9,10},{10,1... | collective-permute-start | bytes 393224 | tf_op jit(solution)/shard_map/ppermute | solution.py:10
  85.8 6.0 %collective-permute-start.4 = (f32[1,2,16384]{2,1,0:T(2,128)S(1)}, f32[1,2,16384]{2,1,0:T(2,128)S(1)}, u32[]{:S(2)}, u32[]{:S(2)}) collective-permute-start(f32[1,2,16384]{2,1,0:T(2,128)S(1)} %constant_dynamic-slice_fusion.1), channel_id=1, source_target_pairs={{0,1},{1,2},{2,3},{3,4},{4,5},{5,6},{6,7},{7,0},{8,9},{9,10},{10,1... | collective-permute-start | bytes 393224 | tf_op jit(solution)/shard_map/ppermute | solution.py:10
  87.5 7.7 %collective-permute-start = (f32[1,2,16384]{2,1,0:T(2,128)S(1)}, f32[1,2,16384]{2,1,0:T(2,128)S(1)}, u32[]{:S(2)}, u32[]{:S(2)}) collective-permute-start(f32[1,2,16384]{2,1,0:T(2,128)S(1)} %constant_dynamic-slice_fusion.2), channel_id=1, source_target_pairs={{0,1},{1,2},{2,3},{3,4},{4,5},{5,6},{6,7},{7,0},{8,9},{9,10},{10,1... | collective-permute-start | bytes 393224 | tf_op jit(solution)/shard_map/ppermute | solution.py:10
  91.2 7.2 %collective-permute-start.9 = (f32[1,2,16384]{2,1,0:T(2,128)S(1)}, f32[1,2,16384]{2,1,0:T(2,128)S(1)}, u32[]{:S(2)}, u32[]{:S(2)}) collective-permute-start(f32[1,2,16384]{2,1,0:T(2,128)S(1)} %broadcast_select_fusion.3), channel_id=1, source_target_pairs={{0,2},{1,3},{2,4},{3,5},{4,6},{5,7},{6,0},{7,1},{8,10},{9,11},{10,... | collective-permute-start | bytes 393224 | tf_op jit(solution)/shard_map/ppermute | solution.py:10
  92.8 8.5 %collective-permute-start.5 = (f32[1,2,16384]{2,1,0:T(2,128)S(1)}, f32[1,2,16384]{2,1,0:T(2,128)S(1)}, u32[]{:S(2)}, u32[]{:S(2)}) collective-permute-start(f32[1,2,16384]{2,1,0:T(2,128)S(1)} %broadcast_select_fusion.4), channel_id=1, source_target_pairs={{0,2},{1,3},{2,4},{3,5},{4,6},{5,7},{6,0},{7,1},{8,10},{9,11},{10,... | collective-permute-start | bytes 393224 | tf_op jit(solution)/shard_map/ppermute | solution.py:10
  95.3 7.5 %collective-permute-start.1 = (f32[1,2,16384]{2,1,0:T(2,128)S(1)}, f32[1,2,16384]{2,1,0:T(2,128)S(1)}, u32[]{:S(2)}, u32[]{:S(2)}) collective-permute-start(f32[1,2,16384]{2,1,0:T(2,128)S(1)} %broadcast_select_fusion.5), channel_id=1, source_target_pairs={{0,2},{1,3},{2,4},{3,5},{4,6},{5,7},{6,0},{7,1},{8,10},{9,11},{10,... | collective-permute-start | bytes 393224 | tf_op jit(solution)/shard_map/ppermute | solution.py:10
  98.5 7.1 %collective-permute-start.10 = (f32[1,2,16384]{2,1,0:T(2,128)S(1)}, f32[1,2,16384]{2,1,0:T(2,128)S(1)}, u32[]{:S(2)}, u32[]{:S(2)}) collective-permute-start(f32[1,2,16384]{2,1,0:T(2,128)S(1)} %broadcast_select_fusion.6), channel_id=1, source_target_pairs={{0,4},{1,5},{2,6},{3,7},{4,0},{5,1},{6,2},{7,3},{8,12},{9,13},{10,... | collective-permute-start | bytes 393224 | tf_op jit(solution)/shard_map/ppermute | solution.py:10
  101.3 7.1 %collective-permute-start.6 = (f32[1,2,16384]{2,1,0:T(2,128)S(1)}, f32[1,2,16384]{2,1,0:T(2,128)S(1)}, u32[]{:S(2)}, u32[]{:S(2)}) collective-permute-start(f32[1,2,16384]{2,1,0:T(2,128)S(1)} %broadcast_select_fusion.7), channel_id=1, source_target_pairs={{0,4},{1,5},{2,6},{3,7},{4,0},{5,1},{6,2},{7,3},{8,12},{9,13},{10,... | collective-permute-start | bytes 393224 | tf_op jit(solution)/shard_map/ppermute | solution.py:10
  102.9 9.0 %collective-permute-start.2 = (f32[1,2,16384]{2,1,0:T(2,128)S(1)}, f32[1,2,16384]{2,1,0:T(2,128)S(1)}, u32[]{:S(2)}, u32[]{:S(2)}) collective-permute-start(f32[1,2,16384]{2,1,0:T(2,128)S(1)} %broadcast_select_fusion.8), channel_id=1, source_target_pairs={{0,4},{1,5},{2,6},{3,7},{4,0},{5,1},{6,2},{7,3},{8,12},{9,13},{10,... | collective-permute-start | bytes 393224 | tf_op jit(solution)/shard_map/ppermute | solution.py:10
  105.8 6.3 %collective-permute-start.11 = (f32[1,1,16384]{2,1,0:T(1,128)S(1)}, f32[1,1,16384]{2,1,0:T(1,128)S(1)}, u32[]{:S(2)}, u32[]{:S(2)}) collective-permute-start(f32[1,1,16384]{2,1,0:T(1,128)S(1)} %get-tuple-element.10), channel_id=1, source_target_pairs={{0,1},{1,2},{2,3},{3,4},{4,5},{5,6},{6,7},{7,0},{8,9},{9,10},{10,1... | collective-permute-start | bytes 196616 | tf_op jit(solution)/shard_map/ppermute | solution.py:10
  108.6 19.7 %collective-permute-start.7 = (f32[1,1,16384]{2,1,0:T(1,128)S(1)}, f32[1,1,16384]{2,1,0:T(1,128)S(1)}, u32[]{:S(2)}, u32[]{:S(2)}) collective-permute-start(f32[1,1,16384]{2,1,0:T(1,128)S(1)} %get-tuple-element.12), channel_id=1, source_target_pairs={{0,1},{1,2},{2,3},{3,4},{4,5},{5,6},{6,7},{7,0},{8,9},{9,10},{10,1... | collective-permute-start | bytes 196616 | tf_op jit(solution)/shard_map/ppermute | solution.py:10
  112.0 32.2 %collective-permute-start.3 = (f32[1,1,16384]{2,1,0:T(1,128)S(1)}, f32[1,1,16384]{2,1,0:T(1,128)S(1)}, u32[]{:S(2)}, u32[]{:S(2)}) collective-permute-start(f32[1,1,16384]{2,1,0:T(1,128)S(1)} %get-tuple-element.14), channel_id=1, source_target_pairs={{0,1},{1,2},{2,3},{3,4},{4,5},{5,6},{6,7},{7,0},{8,9},{9,10},{10,1... | collective-permute-start | bytes 196616 | tf_op jit(solution)/shard_map/ppermute | solution.py:10
Sparse Core Ops, SparseCore 0:
  12.9 70.8 all-reduce.2
where the time goes:
time: 188 us; the launch traced here: 187 us
  waiting for transfers between devices  84.6 us (45%)
  blocking collectives  58.6 us (31%)
  between operations  15 us (8%)
  other arithmetic  13.5 us (7%)
  starting transfers between devices  9.11 us (5%)
  local copies, waits for them, and re-layouts  6.49 us (3%)
    psum x1, waiting for transfers between devices, from_root(): return lax.psum(block, axis)  70.2 us
    all_gather x1, blocking collectives, join_parts(): lax.all_gather(pieces[2], 'inst', axis=2, tiled=True)  16.1 us
    all_gather x1, blocking collectives, join_parts(): lax.all_gather(pieces[1], 'inst', axis=2, tiled=True)  15.8 us
    all_gather x1, blocking collectives, join_parts(): lax.all_gather(pieces[0], 'inst', axis=2, tiled=True)  15 us
    ppermute x12, waiting for transfers between devices, passed_along(): return lax.ppermute(value, axis, pairs)  14.4 us
    psum x1, blocking collectives, grand_total(): return lax.psum(partial_value, 'shard')  11.8 us
    ppermute x12, starting transfers between devices, passed_along(): return lax.ppermute(value, axis, pairs)  9.07 us
    reduce_sum x1, other arithmetic, weighted(): jnp.sum(combined * weights)  4.28 us
  transfers between devices with their start and end apart: 13, of which 8 were waited for; matrix products, arithmetic and copies ran while one was open for 2% of the time, Pallas kernels for 0%

commit v1 on v0

--- a/solution.py
+++ b/solution.py
@@ -2,6 +2,18 @@
 import jax.numpy as jnp
 from jax import lax
 from jax.sharding import PartitionSpec as P
+
+
+def gather_by_bits(array, axis, dim):
+    ways, here, step = (lax.axis_size(axis), lax.axis_index(axis), array.shape[dim])
+    line, have = (array, 1)
+    while have < ways:
+        line = jnp.concatenate(
+            [line, lax.ppermute(line, axis, [(d, (d - have) % ways) for d in range(ways)])],
+            axis=dim,
+        )
+        have = 2 * have
+    return jnp.roll(line, here * step, axis=dim)
 
 
 def passed_along(value, axis, steps):
@@ -36,7 +48,7 @@
     return (
         lax.all_gather(pieces[0], "inst", axis=2, tiled=True),
         lax.all_gather(pieces[1], "inst", axis=2, tiled=True),
-        lax.all_gather(pieces[2], "inst", axis=2, tiled=True),
+        gather_by_bits(pieces[2], "inst", 2),
     )
 
 

time: 188 us -> 185 us (0.984)
  blocking collectives: 58.6 us -> 43.8 us
  waiting for transfers between devices: 84.6 us -> 93.8 us
  starting transfers between devices: 9.11 us -> 11.7 us
    all_gather x1 -> x0, blocking collectives: 16.1 us -> none  [join_parts(): lax.all_gather(pieces[2], 'inst', axis=2, tiled=True)]
    ppermute x0 -> x2, waiting for transfers between devices: none -> 9.15 us  [gather_by_bits(): lax.ppermute(line, axis, [(d, (d - have) % ways) for d in range(ways)])]
    ppermute x0 -> x2, starting transfers between devices: none -> 2.55 us  [gather_by_bits(): lax.ppermute(line, axis, [(d, (d - have) % ways) for d in range(ways)])]
  transfers between devices with their start and end apart: 13 -> 15, of which waited for: 8 -> 9; matrix products, arithmetic and copies ran while one was open for 2% -> 2% of each run, Pallas kernels for 0% -> 0%
where the time goes in v1:
time: 185 us
  waiting for transfers between devices  93.8 us (51%)
  blocking collectives  43.8 us (24%)
  between operations  15.1 us (8%)
  other arithmetic  14.4 us (8%)
  starting transfers between devices  11.7 us (6%)
  local copies, waits for them, and re-layouts  5.8 us (3%)
    psum x1, waiting for transfers between devices, from_root(): return lax.psum(block, axis)  70.2 us
    all_gather x1, blocking collectives, join_parts(): lax.all_gather(pieces[0], 'inst', axis=2, tiled=True)  15.9 us
    all_gather x1, blocking collectives, join_parts(): lax.all_gather(pieces[1], 'inst', axis=2, tiled=True)  15.1 us
    ppermute x12, waiting for transfers between devices, passed_along(): return lax.ppermute(value, axis, pairs)  14.4 us
    psum x1, blocking collectives, grand_total(): return lax.psum(partial_value, 'shard')  12.8 us
    ppermute x2, waiting for transfers between devices, gather_by_bits(): lax.ppermute(line, axis, [(d, (d - have) % ways) for d in range(ways)])  9.15 us
    ppermute x12, starting transfers between devices, passed_along(): return lax.ppermute(value, axis, pairs)  9.07 us
    reduce_sum x1, other arithmetic, weighted(): jnp.sum(combined * weights)  4.88 us
  transfers between devices with their start and end apart: 15, of which 9 were waited for; matrix products, arithmetic and copies ran while one was open for 2% of the time, Pallas kernels for 0%

profile of v1, /device:TPU:0, one launch (start us, length us, event | category | flops | bytes accessed | tf_op | source)
XLA Modules:
  0.0 184.6 jit_solution(14972836048192419077)
XLA Ops:
  9.1 2.1 %broadcast_select_fusion.2 = f32[1,2,65536]{2,1,0:T(2,128)} fusion(f32[1,2,65536]{2,1,0:T(2,128)} %param.5, pred[]{:T(512)S(6)} %eq.25), kind=kLoop, calls=%fused_computation.15 | loop fusion | flops 131072 | bytes 1048577 | tf_op jit(solution)/shard_map/jit(_where)/select_n | solution.py:26
  11.3 1.5 broadcast_select_fusion
  13.7 70.2 %all-reduce.3.cloned.1.call-done = (f32[1,2,65536]{2,1,0:T(2,128)}, f32[1,2,65536]{2,1,0:T(2,128)}, f32[1,2,65536]{2,1,0:T(2,128)}) async-done(((f32[1,2,65536]{2,1,0:T(2,128)}, f32[1,2,65536]{2,1,0:T(2,128)}, f32[1,2,65536]{2,1,0:T(2,128)}), (f32[1,2,65536]{2,1,0:T(2,128)}, f32[1,2,65536]{2,1,0:T(2,128)}, f32[1,2,65536]{2,1,0:T(2,128)})) %all-reduce.3.cloned.1.call-update) | async-done | bytes 1572880 | tf_op jit(solution)/shard_map/psum | solution.py:27
  83.9 1.0 constant_dynamic-slice_fusion.1
  85.8 1.6 collective-permute-start.4
  87.6 2.6 %collective-permute-done.8 = f32[1,2,16384]{2,1,0:T(2,128)S(1)} collective-permute-done((f32[1,2,16384]{2,1,0:T(2,128)S(1)}, f32[1,2,16384]{2,1,0:T(2,128)S(1)}, u32[]{:S(2)}, u32[]{:S(2)}) %collective-permute-start.8) | collective-permute-done | bytes 131104 | tf_op jit(solution)/shard_map/ppermute | solution.py:22
  90.2 1.0 broadcast_select_fusion.3
  91.8 1.0 broadcast_select_fusion.4
  92.8 2.4 %collective-permute-start.5 = (f32[1,2,16384]{2,1,0:T(2,128)S(1)}, f32[1,2,16384]{2,1,0:T(2,128)S(1)}, u32[]{:S(2)}, u32[]{:S(2)}) collective-permute-start(f32[1,2,16384]{2,1,0:T(2,128)S(1)} %broadcast_select_fusion.4), channel_id=1, source_target_pairs={{0,2},{1,3},{2,4},{3,5},{4,6},{5,7},{6,0},{7,1},{8,10},{9,11},{10,... | collective-permute-start | bytes 393224 | tf_op jit(solution)/shard_map/ppermute | solution.py:22
  95.9 2.5 %collective-permute-done.9 = f32[1,2,16384]{2,1,0:T(2,128)S(1)} collective-permute-done((f32[1,2,16384]{2,1,0:T(2,128)S(1)}, f32[1,2,16384]{2,1,0:T(2,128)S(1)}, u32[]{:S(2)}, u32[]{:S(2)}) %collective-permute-start.9) | collective-permute-done | bytes 131104 | tf_op jit(solution)/shard_map/ppermute | solution.py:22
  98.5 1.7 collective-permute-start.10
  100.2 1.0 collective-permute-done.5
  101.3 1.0 collective-permute-start.6
  103.7 1.9 %collective-permute-done.10 = f32[1,2,16384]{2,1,0:T(2,128)S(1)} collective-permute-done((f32[1,2,16384]{2,1,0:T(2,128)S(1)}, f32[1,2,16384]{2,1,0:T(2,128)S(1)}, u32[]{:S(2)}, u32[]{:S(2)}) %collective-permute-start.10) | collective-permute-done | bytes 131104 | tf_op jit(solution)/shard_map/ppermute | solution.py:22
  105.9 2.6 %collective-permute-done.6 = f32[1,2,16384]{2,1,0:T(2,128)S(1)} collective-permute-done((f32[1,2,16384]{2,1,0:T(2,128)S(1)}, f32[1,2,16384]{2,1,0:T(2,128)S(1)}, u32[]{:S(2)}, u32[]{:S(2)}) %collective-permute-start.6) | collective-permute-done | bytes 131104 | tf_op jit(solution)/shard_map/ppermute | solution.py:22
  108.7 3.2 %collective-permute-done.2 = f32[1,2,16384]{2,1,0:T(2,128)S(1)} collective-permute-done((f32[1,2,16384]{2,1,0:T(2,128)S(1)}, f32[1,2,16384]{2,1,0:T(2,128)S(1)}, u32[]{:S(2)}, u32[]{:S(2)}) %collective-permute-start.2) | collective-permute-done | bytes 131104 | tf_op jit(solution)/shard_map/ppermute | solution.py:22
  112.3 1.6 collective-permute-start.12
  113.9 15.1 %all_gather.7 = f32[1,2,65536]{2,1,0:T(2,128)S(1)} all-gather(f32[1,2,16384]{2,1,0:T(2,128)S(1)} %pad_maximum_fusion.2), channel_id=1, replica_groups=mesh['inst'=4,'shard'=8] {'inst'}, dimensions={2}, use_global_device_ids=true | all-gather | bytes 655360 | tf_op jit(solution)/shard_map/all_gather | solution.py:50
  129.2 15.9 %all_gather.6 = f32[1,2,65536]{2,1,0:T(2,128)S(1)} all-gather(f32[1,2,16384]{2,1,0:T(2,128)S(1)} %pad_maximum_fusion.1), channel_id=1, replica_groups=mesh['inst'=4,'shard'=8] {'inst'}, dimensions={2}, use_global_device_ids=true | all-gather | bytes 655360 | tf_op jit(solution)/shard_map/all_gather | solution.py:49
  145.3 1.0 collective-permute-start.13
  146.3 9.1 %collective-permute-done.13 = f32[1,2,32768]{2,1,0:T(2,128)S(1)} collective-permute-done((f32[1,2,32768]{2,1,0:T(2,128)S(1)}, f32[1,2,32768]{2,1,0:T(2,128)S(1)}, u32[]{:S(2)}, u32[]{:S(2)}) %collective-permute-start.13) | collective-permute-done | bytes 262176 | tf_op jit(solution)/shard_map/ppermute | solution.py:12
  155.7 4.9 %fusion.6 = (f32[]{:T(128)}, f32[]{:T(128)}, f32[1,2,65536]{2,1,0:T(2,128)}) fusion(f32[1,2,65536]{2,1,0:T(2,128)S(1)} %all_gather.7, f32[1,2,65536]{2,1,0:T(2,128)S(1)} %all_gather.6, s32[2]{0:T(128)S(1)} %and_select_fusion.2, f32[1,2,131072]{2,1,0:T(2,128)S(1)} %constant_dynamic-update-slice_fusion, s32[]{:T(128)S(6)} %select_n.126), kind=kLoop, calls=%fused_computation.9 | loop fusion | flops 3014654 | bytes 2097172 | tf_op jit(solution)/shard_map/reduce_sum | solution.py:40
  160.6 1.4 pad_maximum_fusion.4
  162.8 12.8 %psum.31 = f32[2]{0:T(128)S(1)} all-reduce(f32[2]{0:T(128)S(1)} %pad_maximum_fusion.4), channel_id=1, replica_groups=mesh['inst'=4,'shard'=8] {'shard'}, use_global_device_ids=true, to_apply=%region_5.6 | all-reduce | flops 2 | bytes 16 | tf_op jit(solution)/shard_map/psum | solution.py:44
  (54 shorter events, 10.4 us)
Async XLA Ops:
  7.2 76.7 %all-reduce.3.cloned.1.call-start = ((), (), s32[]{:S(2)}) async-start(), calls=%async_computation | async-start | bytes 3145728 | tf_op jit(solution)/shard_map/psum | solution.py:27
  7.2 0.7 copy-start.4
  9.1 2.2 %copy-start = (f32[1,2,65536]{2,1,0:T(2,128)S(1)}, f32[1,2,65536]{2,1,0:T(2,128)}, u32[]{:S(2)}) copy-start(f32[1,2,65536]{2,1,0:T(2,128)} %param.7) | copy-start | bytes 1572868
  9.1 2.2 %copy-start.1 = (f32[1,2,65536]{2,1,0:T(2,128)S(1)}, f32[1,2,65536]{2,1,0:T(2,128)}, u32[]{:S(2)}) copy-start(f32[1,2,65536]{2,1,0:T(2,128)} %param.6) | copy-start | bytes 1572868
  12.8 0.7 copy-start.3
  83.9 3.6 %copy-start.2 = (f32[1,2,65536]{2,1,0:T(2,128)S(1)}, f32[1,2,65536]{2,1,0:T(2,128)}, u32[]{:S(2)}) copy-start(f32[1,2,65536]{2,1,0:T(2,128)} %get-tuple-element.7) | copy-start | bytes 1572868
  84.9 5.3 %collective-permute-start.8 = (f32[1,2,16384]{2,1,0:T(2,128)S(1)}, f32[1,2,16384]{2,1,0:T(2,128)S(1)}, u32[]{:S(2)}, u32[]{:S(2)}) collective-permute-start(f32[1,2,16384]{2,1,0:T(2,128)S(1)} %constant_dynamic-slice_fusion.1), channel_id=1, source_target_pairs={{0,1},{1,2},{2,3},{3,4},{4,5},{5,6},{6,7},{7,0},{8,9},{9,10},{10,1... | collective-permute-start | bytes 393224 | tf_op jit(solution)/shard_map/ppermute | solution.py:22
  85.8 6.0 %collective-permute-start.4 = (f32[1,2,16384]{2,1,0:T(2,128)S(1)}, f32[1,2,16384]{2,1,0:T(2,128)S(1)}, u32[]{:S(2)}, u32[]{:S(2)}) collective-permute-start(f32[1,2,16384]{2,1,0:T(2,128)S(1)} %constant_dynamic-slice_fusion.2), channel_id=1, source_target_pairs={{0,1},{1,2},{2,3},{3,4},{4,5},{5,6},{6,7},{7,0},{8,9},{9,10},{10,1... | collective-permute-start | bytes 393224 | tf_op jit(solution)/shard_map/ppermute | solution.py:22
  87.5 7.7 %collective-permute-start = (f32[1,2,16384]{2,1,0:T(2,128)S(1)}, f32[1,2,16384]{2,1,0:T(2,128)S(1)}, u32[]{:S(2)}, u32[]{:S(2)}) collective-permute-start(f32[1,2,16384]{2,1,0:T(2,128)S(1)} %constant_dynamic-slice_fusion.3), channel_id=1, source_target_pairs={{0,1},{1,2},{2,3},{3,4},{4,5},{5,6},{6,7},{7,0},{8,9},{9,10},{10,1... | collective-permute-start | bytes 393224 | tf_op jit(solution)/shard_map/ppermute | solution.py:22
  91.2 7.2 %collective-permute-start.9 = (f32[1,2,16384]{2,1,0:T(2,128)S(1)}, f32[1,2,16384]{2,1,0:T(2,128)S(1)}, u32[]{:S(2)}, u32[]{:S(2)}) collective-permute-start(f32[1,2,16384]{2,1,0:T(2,128)S(1)} %broadcast_select_fusion.3), channel_id=1, source_target_pairs={{0,2},{1,3},{2,4},{3,5},{4,6},{5,7},{6,0},{7,1},{8,10},{9,11},{10,... | collective-permute-start | bytes 393224 | tf_op jit(solution)/shard_map/ppermute | solution.py:22
  92.8 8.5 %collective-permute-start.5 = (f32[1,2,16384]{2,1,0:T(2,128)S(1)}, f32[1,2,16384]{2,1,0:T(2,128)S(1)}, u32[]{:S(2)}, u32[]{:S(2)}) collective-permute-start(f32[1,2,16384]{2,1,0:T(2,128)S(1)} %broadcast_select_fusion.4), channel_id=1, source_target_pairs={{0,2},{1,3},{2,4},{3,5},{4,6},{5,7},{6,0},{7,1},{8,10},{9,11},{10,... | collective-permute-start | bytes 393224 | tf_op jit(solution)/shard_map/ppermute | solution.py:22
  95.3 7.5 %collective-permute-start.1 = (f32[1,2,16384]{2,1,0:T(2,128)S(1)}, f32[1,2,16384]{2,1,0:T(2,128)S(1)}, u32[]{:S(2)}, u32[]{:S(2)}) collective-permute-start(f32[1,2,16384]{2,1,0:T(2,128)S(1)} %broadcast_select_fusion.5), channel_id=1, source_target_pairs={{0,2},{1,3},{2,4},{3,5},{4,6},{5,7},{6,0},{7,1},{8,10},{9,11},{10,... | collective-permute-start | bytes 393224 | tf_op jit(solution)/shard_map/ppermute | solution.py:22
  98.5 7.1 %collective-permute-start.10 = (f32[1,2,16384]{2,1,0:T(2,128)S(1)}, f32[1,2,16384]{2,1,0:T(2,128)S(1)}, u32[]{:S(2)}, u32[]{:S(2)}) collective-permute-start(f32[1,2,16384]{2,1,0:T(2,128)S(1)} %broadcast_select_fusion.6), channel_id=1, source_target_pairs={{0,4},{1,5},{2,6},{3,7},{4,0},{5,1},{6,2},{7,3},{8,12},{9,13},{10,... | collective-permute-start | bytes 393224 | tf_op jit(solution)/shard_map/ppermute | solution.py:22
  101.3 7.1 %collective-permute-start.6 = (f32[1,2,16384]{2,1,0:T(2,128)S(1)}, f32[1,2,16384]{2,1,0:T(2,128)S(1)}, u32[]{:S(2)}, u32[]{:S(2)}) collective-permute-start(f32[1,2,16384]{2,1,0:T(2,128)S(1)} %broadcast_select_fusion.7), channel_id=1, source_target_pairs={{0,4},{1,5},{2,6},{3,7},{4,0},{5,1},{6,2},{7,3},{8,12},{9,13},{10,... | collective-permute-start | bytes 393224 | tf_op jit(solution)/shard_map/ppermute | solution.py:22
  102.9 9.0 %collective-permute-start.2 = (f32[1,2,16384]{2,1,0:T(2,128)S(1)}, f32[1,2,16384]{2,1,0:T(2,128)S(1)}, u32[]{:S(2)}, u32[]{:S(2)}) collective-permute-start(f32[1,2,16384]{2,1,0:T(2,128)S(1)} %broadcast_select_fusion.8), channel_id=1, source_target_pairs={{0,4},{1,5},{2,6},{3,7},{4,0},{5,1},{6,2},{7,3},{8,12},{9,13},{10,... | collective-permute-start | bytes 393224 | tf_op jit(solution)/shard_map/ppermute | solution.py:22
  105.8 6.3 %collective-permute-start.11 = (f32[1,1,16384]{2,1,0:T(1,128)S(1)}, f32[1,1,16384]{2,1,0:T(1,128)S(1)}, u32[]{:S(2)}, u32[]{:S(2)}) collective-permute-start(f32[1,1,16384]{2,1,0:T(1,128)S(1)} %get-tuple-element.13), channel_id=1, source_target_pairs={{0,1},{1,2},{2,3},{3,4},{4,5},{5,6},{6,7},{7,0},{8,9},{9,10},{10,1... | collective-permute-start | bytes 196616 | tf_op jit(solution)/shard_map/ppermute | solution.py:22
  108.6 5.2 %collective-permute-start.7 = (f32[1,1,16384]{2,1,0:T(1,128)S(1)}, f32[1,1,16384]{2,1,0:T(1,128)S(1)}, u32[]{:S(2)}, u32[]{:S(2)}) collective-permute-start(f32[1,1,16384]{2,1,0:T(1,128)S(1)} %get-tuple-element.15), channel_id=1, source_target_pairs={{0,1},{1,2},{2,3},{3,4},{4,5},{5,6},{6,7},{7,0},{8,9},{9,10},{10,1... | collective-permute-start | bytes 196616 | tf_op jit(solution)/shard_map/ppermute | solution.py:22
  112.0 17.1 %collective-permute-start.3 = (f32[1,1,16384]{2,1,0:T(1,128)S(1)}, f32[1,1,16384]{2,1,0:T(1,128)S(1)}, u32[]{:S(2)}, u32[]{:S(2)}) collective-permute-start(f32[1,1,16384]{2,1,0:T(1,128)S(1)} %get-tuple-element.17), channel_id=1, source_target_pairs={{0,1},{1,2},{2,3},{3,4},{4,5},{5,6},{6,7},{7,0},{8,9},{9,10},{10,1... | collective-permute-start | bytes 196616 | tf_op jit(solution)/shard_map/ppermute | solution.py:22
  112.3 32.9 %collective-permute-start.12 = (f32[1,2,16384]{2,1,0:T(2,128)S(1)}, f32[1,2,16384]{2,1,0:T(2,128)S(1)}, u32[]{:S(2)}, u32[]{:S(2)}) collective-permute-start(f32[1,2,16384]{2,1,0:T(2,128)S(1)} %get-tuple-element.11), channel_id=1, source_target_pairs={{0,24},{8,0},{16,8},{24,16},{1,25},{9,1},{17,9},{25,17},{2,26},{10... | collective-permute-start | bytes 393224 | tf_op jit(solution)/shard_map/ppermute | solution.py:12
  145.3 10.1 %collective-permute-start.13 = (f32[1,2,32768]{2,1,0:T(2,128)S(1)}, f32[1,2,32768]{2,1,0:T(2,128)S(1)}, u32[]{:S(2)}, u32[]{:S(2)}) collective-permute-start(f32[1,2,32768]{2,1,0:T(2,128)S(1)} %pad_maximum_fusion), channel_id=1, source_target_pairs={{0,16},{8,24},{16,0},{24,8},{1,17},{9,25},{17,1},{25,9},{2,18},{10... | collective-permute-start | bytes 786440 | tf_op jit(solution)/shard_map/ppermute | solution.py:12
Sparse Core Ops, SparseCore 0:
  12.9 70.8 all-reduce.2
